TPU v7x, 256 devices: a whole 4x4x8 slice. The times are simulated.
256 devices in a mesh: users: 64 (over z, y, core), items: 4 (over x).
Axes of the slice: x: 4, y: 4, z: 8, core: 2. Of those that a mesh axis runs over, the one named last changes fastest.
Arguments:
- user_factor: bfloat16 [131072, 256], P('users'), may hold values from -2.390625 to 2.390625
- hot_factor: bfloat16 [512, 256], replicated, may hold values from -2.390625 to 2.390625
- cold_factor: bfloat16 [65536, 256], P(('users', 'items')), may hold values from -2.390625 to 2.390625
- hour_factor: bfloat16 [168, 256], replicated, may hold values from -2.390625 to 2.390625
- block_user: int32 [256, 512], P(('users', 'items')), may hold values from 0 to 2047
- block_slot: int32 [256, 512], P(('users', 'items')), may hold values from 0 to 159
- block_hour: int32 [256, 512], P(('users', 'items')), may hold values from 0 to 20
- block_count: int32 [256], P(('users', 'items')), may hold values from 128 to 512, as said below
- need_rows: int32 [256, 64, 2], P(('users', 'items')), may hold values from 0 to 15
- observed: bfloat16 [256, 512, 128], P(('users', 'items')), may hold values from 0 to 1, as said below
Outputs:
- user_grad: float32 [131072, 256], P(('users', 'items'))
- cold_grad: float32 [65536, 256], P(('users', 'items'))
- hot_grad: float32 [512, 256], P(('users', 'items'))
- hour_grad: float32 [168, 256], replicated
Inputs may be any that keep to these rules, and one draw needn't show every extreme that they name: `block_count`: some device has all 512 slots live. `observed`: every entry is 0 or 1.
All inputs are finite; a program needn't handle non-finite values.
Results may differ from a plain program's by a relative error of at most 0.0029.
Values may be sent and summed in bfloat16 or wider, within the bound.
A program may use at most 128 MiB of HBM per device.

v0:
```python
import jax
import jax.numpy as jnp
from jax import lax
from jax.sharding import PartitionSpec as P

IB = 16
HB = 8


def body(
    user_factor,
    hot_factor,
    cold_factor,
    hour_factor,
    block_user,
    block_slot,
    block_hour,
    block_count,
    need_rows,
    observed,
):
    rank_size = user_factor.shape[1]
    hour_count = hour_factor.shape[0]
    hour_blocks = hour_count // HB
    hot_rows = hot_factor.shape[0]
    shard_len = cold_factor.shape[0]
    peer_count = lax.axis_size("users")
    requests = need_rows[0]
    offsets = jnp.arange(IB, dtype=jnp.int32)
    gathered = lax.all_gather(cold_factor, "users", axis=0, tiled=True)
    wanted_rows = (
        jnp.arange(peer_count, dtype=jnp.int32)[:, None, None] * shard_len
        + requests[:, :, None] * IB
        + offsets
    ).reshape(-1)
    fetched = gathered[wanted_rows]
    item_table = jnp.concatenate([hot_factor, fetched], axis=0)
    hour_table = hour_factor.reshape(hour_blocks, HB * rank_size)
    block_total = block_user.shape[1]
    group_len = min(block_total, 512)
    groups = block_total // group_len
    live_count = block_count[0]
    data = (
        block_user[0].reshape(groups, group_len),
        block_slot[0].reshape(groups, group_len),
        block_hour[0].reshape(groups, group_len),
        jnp.arange(block_total, dtype=jnp.int32).reshape(groups, group_len),
        observed[0].reshape(groups, group_len, IB, HB),
    )
    block_ids = jnp.arange(hour_blocks, dtype=jnp.int32)

    def one_group(carry, group_data):
        grad_user, grad_item, grad_hour = carry
        users_idx, slots_idx, hours_idx, position, obs = group_data
        user_rows = user_factor[users_idx]
        item_idx = slots_idx[:, None] * IB + offsets
        item_rows = item_table[item_idx]
        hour_onehot = (hours_idx[:, None] == block_ids).astype(jnp.bfloat16)
        hour_rows = jnp.dot(hour_onehot, hour_table, preferred_element_type=jnp.float32)
        hour_rows = hour_rows.astype(jnp.bfloat16).reshape(group_len, HB, rank_size)
        user_item = (
            user_rows.astype(jnp.float32)[:, None, :] * item_rows.astype(jnp.float32)
        ).astype(jnp.bfloat16)
        model = jnp.einsum("gar,gbr->gab", user_item, hour_rows, preferred_element_type=jnp.float32)
        live_mask = position < live_count
        residual = jnp.where(
            live_mask[:, None, None], jax.nn.sigmoid(model) - obs.astype(jnp.float32), 0.0
        )
        residual = residual.astype(jnp.bfloat16)
        weighted = jnp.einsum(
            "gab,gbr->gar", residual, hour_rows, preferred_element_type=jnp.float32
        )
        item_terms = weighted * user_rows.astype(jnp.float32)[:, None, :]
        user_terms = jnp.sum(weighted * item_rows.astype(jnp.float32), axis=1)
        hour_terms = jnp.einsum(
            "gab,gar->gbr", residual, user_item, preferred_element_type=jnp.float32
        )
        grad_user = grad_user.at[users_idx].add(user_terms)
        grad_item = grad_item.at[item_idx.reshape(-1)].add(item_terms.reshape(-1, rank_size))
        grad_hour = grad_hour.at[hours_idx].add(hour_terms.reshape(group_len, HB * rank_size))
        return ((grad_user, grad_item, grad_hour), None)

    start = (
        jnp.zeros((user_factor.shape[0], rank_size), jnp.float32),
        jnp.zeros((item_table.shape[0], rank_size), jnp.float32),
        jnp.zeros((hour_blocks, HB * rank_size), jnp.float32),
    )
    (grad_user, grad_item, grad_hour), _ = lax.scan(one_group, start, data)
    cold_part = grad_item[hot_rows:]
    dense_terms = (
        jnp.zeros((peer_count * shard_len, rank_size), jnp.float32).at[wanted_rows].add(cold_part)
    )
    cold_grad = lax.psum_scatter(dense_terms, "users", scatter_dimension=0, tiled=True)
    hot_grad = lax.psum_scatter(
        grad_item[:hot_rows], ("users", "items"), scatter_dimension=0, tiled=True
    )
    user_grad = lax.psum_scatter(grad_user, "items", scatter_dimension=0, tiled=True)
    hour_grad = lax.psum(grad_hour, ("users", "items")).reshape(hour_count, rank_size)
    return (user_grad, cold_grad, hot_grad, hour_grad)


def solution(mesh):
    in_specs = (
        P("users", None),
        P(),
        P(("users", "items"), None),
        P(),
        P(("users", "items"), None),
        P(("users", "items"), None),
        P(("users", "items"), None),
        P(("users", "items")),
        P(("users", "items"), None, None),
        P(("users", "items"), None, None),
    )
    out_specs = (
        P(("users", "items"), None),
        P(("users", "items"), None),
        P(("users", "items"), None),
        P(),
    )
    return jax.shard_map(body, mesh=mesh, in_specs=in_specs, out_specs=out_specs, check_vma=False)
```

profile of v0, /device:TPU:1, one launch (start us, length us, event | category | flops | bytes accessed | tf_op | source)
XLA Modules:
  0.0 699.8 jit_solution(4450357891006991247)
XLA Ops:
  7.2 0.7 all-gather.2.cloned.1.call-update
  8.6 0.7 bitcast_add_fusion
  9.5 0.1 add.165
  9.7 1.0 reshape.237
  10.7 1.0 copy.19
  11.7 0.7 compare_select_fusion.4
  12.4 2.0 gather_fusion
  14.4 0.1 iota_add_fusion
  14.6 0.1 add.175
  14.7 0.1 compare_select_fusion
  15.0 2.0 copy.20
  17.0 0.8 convolution_convert_fusion
  17.8 2.1 copy.21
  19.9 78.1 %all-gather.2.cloned.1.call-done = bf16[16384,256]{1,0:T(8,128)(2,1)} async-done(((bf16[256,256]{1,0:T(8,128)(2,1)}), bf16[16384,256]{1,0:T(8,128)(2,1)}) %all-gather.2.cloned.1.call-update) | async-done | bytes 8388624 | tf_op jit(solution)/shard_map/all_gather | solution.py:30
  98.0 11.1 %gather_fusion.1 = bf16[2048,256]{1,0:T(8,128)(2,1)S(1)} fusion(bf16[16384,256]{1,0:T(8,128)(2,1)} %all-gather.2.cloned.1.call-done, s32[2048]{0:T(1024)S(1)} %broadcast_clamp_fusion.1), kind=kCustom, calls=%fused_computation.1 | custom fusion | bytes 2105344 | tf_op jit(solution)/shard_map/gather | solution.py:36
  109.2 32.9 %gather_fusion.2 = bf16[8192,256]{1,0:T(8,128)(2,1)} fusion(bf16[2560,256]{1,0:T(8,128)(2,1)S(1)} %pad_maximum_fusion, s32[8192]{0:T(1024)S(1)} %broadcast_clamp_fusion), kind=kCustom, calls=%fused_computation.2 | custom fusion | bytes 8421376 | tf_op jit(solution)/shard_map/while/body/eval_jaxpr/gather | solution.py:57
  142.1 5.0 select_convert_fusion
  147.2 1.0 fusion.4
  148.1 0.6 copy-done.3
  148.8 5.1 broadcast_multiply_fusion
  153.9 3.9 copy.22
  157.8 8.7 %scatter_custom_fusion.3 = f32[21,2048]{1,0:T(8,128)S(1)} fusion(s32[512]{0:T(512)S(1)} %bitcast.48, f32[512,2048]{1,0:T(8,128)} %bitcast.39, f32[]{:T(128)} %constant.13.clone.1), kind=kCustom, calls=%fused_computation.30 | custom fusion | flops 1048576 | bytes 172544 | tf_op jit(solution)/shard_map/while/body/eval_jaxpr/scatter-add | solution.py:80
  166.5 0.7 reshape.241
  167.2 46.2 %scatter_custom_fusion.1 = f32[2560,256]{1,0:T(8,128)} fusion(s32[8192]{0:T(1024)S(1)} %bitcast.40, f32[8192,256]{1,0:T(8,128)} %bitcast.35, f32[]{:T(128)} %constant.13.clone.1), kind=kCustom, calls=%fused_computation.20 | custom fusion | flops 2097152 | bytes 2621952 | tf_op jit(solution)/shard_map/while/body/eval_jaxpr/scatter-add | solution.py:79
  213.4 1.9 slice.15
  215.4 4.9 scatter_custom_fusion
  220.4 18.9 %scatter_custom_fusion.2 = f32[16384,256]{1,0:T(8,128)} fusion(s32[2048]{0:T(1024)S(1)} %bitcast.42, f32[]{:T(128)} %constant.13.clone.1, f32[2560,256]{1,0:T(8,128)} %scatter_custom_fusion.1), kind=kCustom, calls=%fused_computation.11 | custom fusion | flops 524288 | bytes 18874880 | tf_op jit(solution)/shard_map/scatter-add | solution.py:91
  239.3 227.1 %all-reduce.4.cloned.1.call-done = (f32[512,256]{1,0:T(8,128)}, f32[168,256]{1,0:T(8,128)}) async-done(((f32[512,256]{1,0:T(8,128)}, f32[168,256]{1,0:T(8,128)}), (f32[512,256]{1,0:T(8,128)}, f32[168,256]{1,0:T(8,128)})) %all-reduce.4.cloned.1.call-update) | async-done | bytes 696336
  466.4 1.3 constant_dynamic-slice_fusion
  467.7 33.4 %reduce-scatter.3.cloned.1.call-done = f32[512,256]{1,0:T(8,128)} async-done(((f32[2048,256]{1,0:T(8,128)}), f32[512,256]{1,0:T(8,128)}) %reduce-scatter.3.cloned.1.call-update) | async-done | bytes 524304 | tf_op jit(solution)/shard_map/reduce_scatter | solution.py:97
  501.1 190.6 %reduce-scatter.5.cloned.1.call-done = f32[256,256]{1,0:T(8,128)} async-done(((f32[16384,256]{1,0:T(8,128)}), f32[256,256]{1,0:T(8,128)}) %reduce-scatter.5.cloned.1.call-update) | async-done | bytes 262160 | tf_op jit(solution)/shard_map/reduce_scatter | solution.py:93
  691.7 1.6 copy.26
  (35 shorter events, 0.8 us)
Async XLA Ops:
  7.2 5.2 copy-start
  7.2 7.2 %copy-start.6 = (s32[1,512]{1,0:T(1,128)S(1)}, s32[1,512]{1,0:T(1,128)}, u32[]{:S(2)}) copy-start(s32[1,512]{1,0:T(1,128)} %param.15) | copy-start | bytes 6148
  7.2 90.8 %all-gather.2.cloned.1.call-start = ((), (), s32[]{:S(2)}) async-start(), calls=%async_computation.2 | async-start | bytes 8519680 | tf_op jit(solution)/shard_map/all_gather | solution.py:30
  7.9 458.5 %all-reduce.4.cloned.1.call-start = ((), (), s32[]{:S(2)}) async-start(), calls=%async_computation.5 | async-start | bytes 1392640
  14.3 2.7 copy-start.5
  19.9 89.2 %copy-start.4 = (bf16[512,256]{1,0:T(8,128)(2,1)S(1)}, bf16[512,256]{1,0:T(8,128)(2,1)}, u32[]{:S(2)}) copy-start(bf16[512,256]{1,0:T(8,128)(2,1)} %param.11) | copy-start | bytes 786436
  142.1 5.0 copy-start.2
  147.2 1.6 copy-start.3
  215.3 285.7 %reduce-scatter.3.cloned.1.call-start = ((), (), s32[]{:S(2)}) async-start(), calls=%async_computation.3 | async-start | bytes 2621440 | tf_op jit(solution)/shard_map/reduce_scatter | solution.py:97
  220.3 471.3 %reduce-scatter.5.cloned.1.call-start = ((), (), s32[]{:S(2)}) async-start(), calls=%async_computation.4 | async-start | bytes 17039360 | tf_op jit(solution)/shard_map/reduce_scatter | solution.py:93
  239.3 454.0 %copy-start.1 = (bf16[2048,256]{1,0:T(8,128)(2,1)S(1)}, bf16[2048,256]{1,0:T(8,128)(2,1)}, u32[]{:S(2)}) copy-start(bf16[2048,256]{1,0:T(8,128)(2,1)} %param.10) | copy-start | bytes 3145732
Sparse Core Ops, SparseCore 0:
  10.8 87.1 all-gather.1
  215.5 250.8 all-reduce.3
  469.5 31.4 reduce-scatter.2
  506.0 185.6 reduce-scatter.4
where the time goes:
time: 703 us; the launch traced here: 700 us
  waiting for transfers between devices  530 us (75%)
  other arithmetic  80.7 us (11%)
  local copies, waits for them, and re-layouts  62.6 us (9%)
  between operations  14.7 us (2%)
  matrix products  11.9 us (2%)
    unnamed x5, waiting for transfers between devices  228 us
    reduce_scatter x1, waiting for transfers between devices, body(): lax.psum_scatter(dense_terms, 'users', scatter_dimension=0, tiled=True)  191 us
    all_gather x1, waiting for transfers between devices, body(): gathered = lax.all_gather(cold_factor, 'users', axis=0, tiled=True)  78.1 us
    scatter-add x1, other arithmetic, one_group(): grad_item.at[item_idx.reshape(-1)].add(item_terms.reshape(-1, rank_size))  46.2 us
    reduce_scatter x1, waiting for transfers between devices, body(): lax.psum_scatter(grad_user, 'items', scatter_dimension=0, tiled=True)  33.4 us
    gather x1, local copies, waits for them, and re-layouts, one_group(): item_rows = item_table[item_idx]  32.9 us
    scatter-add x1, other arithmetic, body(): jnp.zeros((peer_count * shard_len, rank_size), jnp.float32).at[wanted_rows]  18.9 us
  transfers between devices with their start and end apart: 4, of which 4 were waited for; matrix products, arithmetic and copies ran while one was open for 5% of the time, Pallas kernels for 0%

commit v1 on v0

v1 whole, which is shorter than its diff:
```python
import functools

import jax
import jax.numpy as jnp
from jax import lax
from jax.experimental import pallas as pl
from jax.experimental.pallas import tpu as pltpu
from jax.sharding import PartitionSpec as P

IB = 16
HB = 8
REQ = 2
MESH = pl.DeviceIdType.MESH
F32 = jnp.float32
BF16 = jnp.bfloat16


def dot(a, b, ca=1, cb=0):
    return lax.dot_general(a, b, (((ca,), (cb,)), ((), ())), preferred_element_type=F32)


def onehot(mask):
    return jnp.where(mask, 1.0, 0.0).astype(BF16)


def halves(x):
    hi = x.astype(BF16)
    return hi, (x - hi.astype(F32)).astype(BF16)


def kernel(
    nu,
    ni,
    user_ref,
    hot_ref,
    cold_ref,
    hour_ref,
    bu_ref,
    bs_ref,
    bh_ref,
    cnt_ref,
    need_ref,
    obs_ref,
    ugrad_ref,
    cgrad_ref,
    hgrad_ref,
    tgrad_ref,
    idx_send,
    idx_recv,
    perm,
    row_send,
    row_recv,
    tab,
    urows,
    sel,
    sel_t,
    hours,
    obs_t,
    hour_acc,
    uterm,
    cold32,
    cold_send,
    cold_recv,
    user32,
    user_send,
    user_recv,
    xs_send,
    xs_recv,
    st2,
    st2_send,
    st2_recv,
    hall,
    hflat,
    sems,
):
    p = lax.axis_index("users")
    q = lax.axis_index("items")
    nblk = bu_ref.shape[1]
    users = user_ref.shape[0]
    udev = users // ni
    hot_rows, rank = hot_ref.shape
    cold_rows = cold_ref.shape[0]
    hot_slots = hot_rows // IB
    cold_slots = nu * REQ
    slots = hot_slots + cold_slots
    hour_count = hour_ref.shape[0]
    hour_blocks = hour_count // HB
    hp = hours.shape[0]

    def peer(i):
        h = i // 2 + 1
        return (p + h + (i % 2) * (nu - 2 * h)) % nu

    def copy_users(src, dst, n, to):
        return pltpu.make_async_remote_copy(
            src_ref=src,
            dst_ref=dst,
            send_sem=sems.at[n, 0],
            recv_sem=sems.at[n, 1],
            device_id=(to, q),
            device_id_type=MESH,
        )

    def copy_items(src, dst, n, to):
        return pltpu.make_async_remote_copy(
            src_ref=src,
            dst_ref=dst,
            send_sem=sems.at[n, 0],
            recv_sem=sems.at[n, 1],
            device_id=(p, to),
            device_id_type=MESH,
        )

    def send_users(src, dst, n, lo=0, hi=nu - 1):
        def one(i, c):
            to = peer(i)
            copy_users(src.at[to], dst.at[p], n, to).start()
            return c

        lax.fori_loop(lo, hi, one, 0)

    def wait_users(src, dst, n):
        d = copy_users(src.at[pl.ds(0, nu - 1)], dst.at[pl.ds(0, nu - 1)], n, (p + 1) % nu)
        d.wait_send()
        d.wait_recv()

    def send_items(src, dst, n, k):
        to = (q + k) % ni
        copy_items(src.at[to], dst.at[q], n, to).start()

    def wait_items(src, dst, n):
        d = copy_items(src.at[pl.ds(0, ni - 1)], dst.at[pl.ds(0, ni - 1)], n, (q + 1) % ni)
        d.wait_send()
        d.wait_recv()

    x_order = sorted(range(1, ni), key=lambda k: min(k, ni - k))

    barrier = pltpu.get_barrier_semaphore()

    def greet(i, c):
        pl.semaphore_signal(barrier, inc=1, device_id=(peer(i), q), device_id_type=MESH)
        return c

    lax.fori_loop(0, nu - 1, greet, 0)
    for k in range(1, ni):
        pl.semaphore_signal(barrier, inc=1, device_id=(p, (q + k) % ni), device_id_type=MESH)

    need = need_ref[0]
    lane = lax.broadcasted_iota(jnp.int32, (nu, 128), 1)
    wanted = jnp.where((lane // IB) % REQ == 0, need[:, 0:1], need[:, 1:2]) * IB + lane % IB + 1
    msg = jnp.where(lane // (IB * REQ) == p % 4, wanted, 0)
    for e in range(nu):
        idx_send[e] = msg[e : e + 1, :]

    for h in range(rank // 128):
        tab[h, pl.ds(0, hot_rows), :] = hot_ref[:, h * 128 : (h + 1) * 128].astype(F32)
    hours[...] = jnp.zeros_like(hours)
    hours[pl.ds(0, hour_count), :] = hour_ref[...]
    obs_t[...] = jnp.transpose(obs_ref[0].astype(F32))
    slot_col = jnp.transpose(jnp.broadcast_to(bs_ref[...], (8, nblk)))[:, 0:1]
    user_col = jnp.transpose(jnp.broadcast_to(bu_ref[...], (8, nblk)))[:, 0:1]
    sel[...] = onehot(lax.broadcasted_iota(jnp.int32, (nblk, slots), 1) == slot_col)
    sel_t[...] = onehot(lax.broadcasted_iota(jnp.int32, (slots, nblk), 0) == bs_ref[...])
    urows[...] = jnp.zeros_like(urows)

    def pick_user(c, carry):
        first = pl.multiple_of(c * 256, 256)
        mask = lax.broadcasted_iota(jnp.int32, (nblk, 256), 1) + first == user_col
        urows[...] += dot(onehot(mask), user_ref[pl.ds(first, 256), :])
        return carry

    lax.fori_loop(0, users // 256, pick_user, 0)

    pl.semaphore_wait(barrier, nu - 1 + ni - 1)

    send_users(idx_send, idx_recv, 0)
    idx_recv[pl.ds(p, 1)] = idx_send[pl.ds(p, 1)]
    uterm[...] = jnp.zeros_like(uterm)
    hour_acc[...] = jnp.zeros_like(hour_acc)
    wait_users(idx_send, idx_recv, 0)

    def build(g, c):
        v = idx_recv[4 * g] + idx_recv[4 * g + 1] + idx_recv[4 * g + 2] + idx_recv[4 * g + 3]
        m = onehot(lax.broadcasted_iota(jnp.int32, (cold_rows, 128), 0) + 1 == v)
        perm[g] = m
        rows = dot(m, cold_ref[...], 0, 0).astype(BF16)
        row_send[pl.ds(4 * g, 4)] = rows.reshape(4, IB * REQ, rank)
        return c

    lax.fori_loop(0, nu // 4, build, 0)

    send_users(row_send, row_recv, 1)
    row_recv[pl.ds(p, 1)] = row_send[pl.ds(p, 1)]
    wait_users(row_send, row_recv, 1)
    for h in range(rank // 128):
        tab[h, pl.ds(hot_rows, cold_slots * IB), :] = (
            row_recv[:, :, h * 128 : (h + 1) * 128].reshape(cold_slots * IB, 128).astype(F32)
        )

    hb = jnp.broadcast_to(bh_ref[...], (HB, nblk))
    live = lax.broadcasted_iota(jnp.int32, (HB, nblk), 1) < cnt_ref[0]

    def position(a, c):
        at = [tab[h, pl.ds(a, slots, stride=IB), :] for h in range(rank // 128)]
        items = dot(sel[...], jnp.concatenate(at, axis=1).astype(BF16))
        u = urows[...]
        ui = (u * items).astype(BF16)
        h = hours[...]
        scores = dot(h, ui, 1, 1)
        model = jnp.zeros((HB, nblk), F32)
        for k in range(hour_blocks):
            model = jnp.where(hb == k, scores[k * HB : (k + 1) * HB, :], model)
        seen = obs_t[pl.ds(pl.multiple_of(a * HB, HB), HB), :]
        residual = jnp.where(live, jax.nn.sigmoid(model) - seen, 0.0)
        pieces = [jnp.where(hb == k, residual, 0.0) for k in range(hour_blocks)]
        pieces += [jnp.zeros((HB, nblk), F32)] * (hp // HB - hour_blocks)
        spread = jnp.concatenate(pieces, axis=0).astype(BF16)
        hour_acc[pl.ds(0, hp), :] += dot(spread, ui)
        w = dot(spread, h, 0, 0)
        uterm[...] += w * items
        hi, lo = halves(w * u)
        g = dot(sel_t[...], hi) + dot(sel_t[...], lo)
        first = pl.multiple_of(((a // 8) * 2 + a % 2) * hot_slots, hot_slots)
        xs_send[(a % 8) // 2, pl.ds(first, hot_slots), :] = g[:hot_slots].astype(BF16)
        for k in range(rank // 128):
            cold32[k, pl.ds(a, cold_slots, stride=IB), :] = g[
                hot_slots:, k * 128 : (k + 1) * 128
            ]
        return c

    lax.fori_loop(0, IB, position, 0)

    per_q = rank // ni
    hot_q = hot_rows // ni
    xs_send[:, pl.ds(hot_q, per_q), :] = (
        jnp.transpose(hour_acc[...]).astype(BF16).reshape(ni, per_q, rank)
    )
    for k in range(rank // 128):
        cold_send[:, :, k * 128 : (k + 1) * 128] = (
            cold32[k].astype(BF16).reshape(nu, REQ * IB, 128)
        )
    for k in x_order:
        send_items(xs_send, xs_recv, 2, k)
    send_users(cold_send, cold_recv, 3, 0, nu // 2)

    hi, lo = halves(uterm[...])
    for c in range(ni):
        m = onehot(lax.broadcasted_iota(jnp.int32, (udev, nblk), 0) + c * udev == bu_ref[...])
        user32[c] = dot(m, hi) + dot(m, lo)
        user_send[c] = user32[c].astype(BF16)
    for k in x_order:
        send_items(user_send, user_recv, 4, k)

    xs_recv[pl.ds(q, 1)] = xs_send[pl.ds(q, 1)]
    wait_items(xs_send, xs_recv, 2)
    x1 = xs_recv[0].astype(F32)
    for k in range(1, ni):
        x1 = x1 + xs_recv[k].astype(F32)
    for half in range(2):
        for j in range(2):
            first = (half * 2 + j) * hot_slots
            for k in range(rank // 128):
                st2[j * (rank // 128) + k, pl.ds(half, hot_slots, stride=2), :] = x1[
                    first : first + hot_slots, k * 128 : (k + 1) * 128
                ]
    for k in range(rank // 128):
        st2[2 * (rank // 128) + k] = x1[hot_q : hot_q + per_q, k * 128 : (k + 1) * 128]
    for k in range(3 * rank // 128):
        for e in range(nu):
            st2_send[e, :, k * 128 : (k + 1) * 128] = st2[k, e : e + 1, :]
    send_users(st2_send, st2_recv, 5)
    send_users(cold_send, cold_recv, 3, nu // 2, nu - 1)
    st2_recv[pl.ds(p, 1)] = st2_send[pl.ds(p, 1)]
    cold_recv[pl.ds(p, 1)] = cold_send[pl.ds(p, 1)]
    wait_users(st2_send, st2_recv, 5)
    total = st2_recv[0]
    for e in range(1, nu):
        total = total + st2_recv[e]
    hgrad_ref[pl.ds(0, 1), :] = total[:, :rank]
    hgrad_ref[pl.ds(1, 1), :] = total[:, rank : 2 * rank]
    hall[q, pl.ds(p, 1)] = total[:, 2 * rank :].reshape(1, 1, rank)

    def tell(i, c):
        to = peer(i)
        copy_users(hall.at[q, p], hall.at[q, p], 6, to).start()
        return c

    lax.fori_loop(0, nu - 1, tell, 0)

    wait_items(user_send, user_recv, 4)
    user_recv[pl.ds(q, 1)] = jnp.zeros((1, udev, rank), BF16)
    grad = user32[q]
    for k in range(ni):
        grad = grad + user_recv[k].astype(F32)
    ugrad_ref[...] = grad

    wait_users(hall.at[q], hall.at[q], 6)
    for k in x_order:
        to = (q + k) % ni
        copy_items(hall.at[q], hall.at[q], 7, to).start()

    wait_users(cold_send, cold_recv, 3)
    acc = jnp.zeros((cold_rows, rank), F32)
    for g in range(nu // 4):
        acc = acc + dot(perm[g], cold_recv[pl.ds(4 * g, 4)].reshape(128, rank))
    cgrad_ref[...] = acc

    wait_items(hall, hall, 7)
    for c in range(ni):
        for e in range(nu):
            hflat[pl.ds(c * nu + e, 1), :] = hall[c, e]
    tgrad_ref[...] = jnp.transpose(hflat[...])[:hour_count, :]


def solution(mesh):
    nu, ni = mesh.shape["users"], mesh.shape["items"]

    def body(
        user_factor,
        hot_factor,
        cold_factor,
        hour_factor,
        block_user,
        block_slot,
        block_hour,
        block_count,
        need_rows,
        observed,
    ):
        users, rank = user_factor.shape
        hot_rows = hot_factor.shape[0]
        cold_rows = cold_factor.shape[0]
        hour_count = hour_factor.shape[0]
        nblk = block_user.shape[1]
        slots = hot_rows // IB + nu * REQ
        udev = users // ni
        hp = -(-hour_count // 16) * 16
        part = REQ * IB
        vmem = pl.BlockSpec(memory_space=pltpu.VMEM)
        specs = [vmem] * 10
        specs[7] = pl.BlockSpec(memory_space=pltpu.SMEM)
        small = (hot_rows + rank) // ni
        return pl.pallas_call(
            functools.partial(kernel, nu, ni),
            out_shape=(
                jax.ShapeDtypeStruct((udev, rank), F32),
                jax.ShapeDtypeStruct((cold_rows, rank), F32),
                jax.ShapeDtypeStruct((hot_rows // (nu * ni), rank), F32),
                jax.ShapeDtypeStruct((hour_count, rank), F32),
            ),
            in_specs=specs,
            out_specs=(vmem,) * 4,
            scratch_shapes=[
                pltpu.VMEM((nu, 1, 128), jnp.int32),
                pltpu.VMEM((nu, 1, 128), jnp.int32),
                pltpu.VMEM((nu // 4, cold_rows, 128), BF16),
                pltpu.VMEM((nu, part, rank), BF16),
                pltpu.VMEM((nu, part, rank), BF16),
                pltpu.VMEM((rank // 128, slots * IB, 128), F32),
                pltpu.VMEM((nblk, rank), F32),
                pltpu.VMEM((nblk, slots), BF16),
                pltpu.VMEM((slots, nblk), BF16),
                pltpu.VMEM((hp, rank), BF16),
                pltpu.VMEM((IB * HB, nblk), F32),
                pltpu.VMEM((rank, rank), F32),
                pltpu.VMEM((nblk, rank), F32),
                pltpu.VMEM((rank // 128, nu * part, 128), F32),
                pltpu.VMEM((nu, part, rank), BF16),
                pltpu.VMEM((nu, part, rank), BF16),
                pltpu.VMEM((ni, udev, rank), F32),
                pltpu.VMEM((ni, udev, rank), BF16),
                pltpu.VMEM((ni, udev, rank), BF16),
                pltpu.VMEM((ni, small, rank), BF16),
                pltpu.VMEM((ni, small, rank), BF16),
                pltpu.VMEM((3 * rank // 128, nu, 128), F32),
                pltpu.VMEM((nu, 1, 3 * rank), F32),
                pltpu.VMEM((nu, 1, 3 * rank), F32),
                pltpu.VMEM((ni, nu, 1, rank), F32),
                pltpu.VMEM((rank, rank), F32),
                pltpu.SemaphoreType.DMA((8, 2)),
            ],
            compiler_params=pltpu.CompilerParams(
                collective_id=0, has_side_effects=True, vmem_limit_bytes=56 * 1024 * 1024
            ),
        )(
            user_factor,
            hot_factor,
            cold_factor,
            hour_factor,
            block_user,
            block_slot,
            block_hour,
            block_count,
            need_rows,
            observed,
        )

    in_specs = (
        P("users", None),
        P(),
        P(("users", "items"), None),
        P(),
        P(("users", "items"), None),
        P(("users", "items"), None),
        P(("users", "items"), None),
        P(("users", "items")),
        P(("users", "items"), None, None),
        P(("users", "items"), None, None),
    )
    out_specs = (
        P(("users", "items"), None),
        P(("users", "items"), None),
        P(("users", "items"), None),
        P(),
    )
    return jax.shard_map(body, mesh=mesh, in_specs=in_specs, out_specs=out_specs, check_vma=False)
```

time: 703 us -> 114 us (0.16)
  waiting for transfers between devices: 530 us -> 0 us
  Pallas kernels: 0 us -> 106 us
  other arithmetic: 80.7 us -> 0 us
  local copies, waits for them, and re-layouts: 62.6 us -> 4.59 us
  between operations: 14.7 us -> 1.32 us
  matrix products: 11.9 us -> 0 us
    unnamed x5 -> x0, waiting for transfers between devices: 228 us -> none
    reduce_scatter x2 -> x0, waiting for transfers between devices: 224 us -> none  [the longest x1 191 us: body(): lax.psum_scatter(dense_terms, 'users', scatter_dimension=0, tiled=True)]
    pallas_call x0 -> x1, Pallas kernels: none -> 106 us  [body(): pl.pallas_call(functools.partial(kernel, nu, ni), out_shape=(jax.ShapeDty...]
    scatter-add x4 -> x0, other arithmetic: 78.7 us -> none  [the longest x1 46.2 us: one_group(): grad_item.at[item_idx.reshape(-1)].add(item_terms.reshape(-1, rank_size))]
    all_gather x1 -> x0, waiting for transfers between devices: 78.1 us -> none  [body(): gathered = lax.all_gather(cold_factor, 'users', axis=0, tiled=True)]
    gather x3 -> x0, local copies, waits for them, and re-layouts: 46 us -> none  [the longest x1 32.9 us: one_group(): item_rows = item_table[item_idx]]
    dot_general x4 -> x0, matrix products: 11.9 us -> none  [the longest x1 5.13 us: one_group(): jnp.einsum('gab,gbr->gar', residual, hour_rows, preferred_element_type=jn...]
  transfers between devices with their start and end apart: 4 -> 0, of which waited for: 4 -> 0; matrix products, arithmetic and copies ran while one was open for 5% -> 0% of each run, Pallas kernels for 0% -> 0%
where the time goes in v1:
time: 114 us; the launch traced here: 112 us
  Pallas kernels  106 us (93%)
  local copies, waits for them, and re-layouts  4.59 us (4%)
  between operations  1.32 us (1%)
    pallas_call x1, Pallas kernels, body(): pl.pallas_call(functools.partial(kernel, nu, ni), out_shape=(jax.ShapeDty...  106 us
    unnamed x13, local copies, waits for them, and re-layouts  4.59 us

profile of v1, /device:TPU:1, one launch (start us, length us, event | category | flops | bytes accessed | tf_op | source)
XLA Modules:
  0.0 112.3 jit_solution(3397081748255350191)
XLA Ops:
  0.6 0.0 copy-start.3
  1.3 0.0 copy-done.3
  1.3 0.7 copy.14.need_ref
  2.0 106.4 %shard_map.129 = (f32[512,256]{1,0:T(8,128)}, f32[256,256]{1,0:T(8,128)}, f32[2,256]{1,0:T(2,128)}, f32[168,256]{1,0:T(8,128)}) custom-call(bf16[2048,256]{1,0:T(8,128)(2,1)} %user_ref.1, bf16[512,256]{1,0:T(8,128)(2,1)} %hot_ref.1, bf16[256,256]{1,0:T(8,128)(2,1)} %cold_ref.1, bf16[168,256]{1,0:T(8,128)(2,1)} %hour_ref.1, s32[1,512]{1,0:T(1,128)} %bu_ref.1, ...), custom_call_target="tpu_custom_call" | custom-call | tf_op jit(solution)/shard_map/pallas_call | solution.py:343
  108.4 0.0 copy-start
  108.4 1.9 %copy.20 = f32[512,256]{1,0:T(8,128)} copy(f32[512,256]{1,0:T(8,128)} %get-tuple-element.8) | data formatting | bytes 1048576
  110.3 0.0 copy-done
  110.3 0.0 copy-start.2
  110.3 0.0 copy-start.1
  110.3 0.7 copy.21
  111.0 0.0 copy-done.2
  111.0 0.6 copy.22
  111.6 0.0 copy-done.1
  111.6 0.7 copy.23
Async XLA Ops:
  0.6 0.7 copy-start.3
  108.4 1.9 %copy-start = (f32[256,256]{1,0:T(8,128)S(1)}, f32[256,256]{1,0:T(8,128)}, u32[]{:S(2)}) copy-start(f32[256,256]{1,0:T(8,128)} %get-tuple-element.9) | copy-start | bytes 786436
  110.3 0.7 copy-start.2
  110.3 1.3 %copy-start.1 = (f32[168,256]{1,0:T(8,128)S(1)}, f32[168,256]{1,0:T(8,128)}, u32[]{:S(2)}) copy-start(f32[168,256]{1,0:T(8,128)} %get-tuple-element.11) | copy-start | bytes 516100

commit v2 on v1

--- a/solution.py
+++ b/solution.py
@@ -10,6 +10,10 @@
 IB = 16
 HB = 8
 REQ = 2
+CH = 4
+POS = IB // CH
+EARLY = 2
+ROWS = REQ * POS
 MESH = pl.DeviceIdType.MESH
 F32 = jnp.float32
 BF16 = jnp.bfloat16
@@ -50,6 +54,7 @@
     perm,
     row_send,
     row_recv,
+    hot_tab,
     tab,
     urows,
     sel,
@@ -145,15 +150,16 @@
     for k in range(1, ni):
         pl.semaphore_signal(barrier, inc=1, device_id=(p, (q + k) % ni), device_id_type=MESH)
 
+    span = 128 // ROWS
     need = need_ref[0]
     lane = lax.broadcasted_iota(jnp.int32, (nu, 128), 1)
-    wanted = jnp.where((lane // IB) % REQ == 0, need[:, 0:1], need[:, 1:2]) * IB + lane % IB + 1
-    msg = jnp.where(lane // (IB * REQ) == p % 4, wanted, 0)
+    wanted = jnp.where((lane // POS) % REQ == 0, need[:, 0:1], need[:, 1:2]) * IB + lane % POS + 1
+    msg = jnp.where(lane // ROWS == p % span, wanted, 0)
     for e in range(nu):
         idx_send[e] = msg[e : e + 1, :]
 
     for h in range(rank // 128):
-        tab[h, pl.ds(0, hot_rows), :] = hot_ref[:, h * 128 : (h + 1) * 128].astype(F32)
+        hot_tab[h] = hot_ref[:, h * 128 : (h + 1) * 128].astype(F32)
     hours[...] = jnp.zeros_like(hours)
     hours[pl.ds(0, hour_count), :] = hour_ref[...]
     obs_t[...] = jnp.transpose(obs_ref[0].astype(F32))
@@ -179,29 +185,41 @@
     hour_acc[...] = jnp.zeros_like(hour_acc)
     wait_users(idx_send, idx_recv, 0)
 
-    def build(g, c):
-        v = idx_recv[4 * g] + idx_recv[4 * g + 1] + idx_recv[4 * g + 2] + idx_recv[4 * g + 3]
-        m = onehot(lax.broadcasted_iota(jnp.int32, (cold_rows, 128), 0) + 1 == v)
-        perm[g] = m
+    groups = nu // span
+
+    def build(i, carry):
+        c = i // groups
+        g = i % groups
+        first = pl.multiple_of(g * span, span)
+        v = jnp.sum(idx_recv[pl.ds(first, span)], axis=0) - 1 + c * POS
+        m = onehot(lax.broadcasted_iota(jnp.int32, (cold_rows, 128), 0) == v)
+        perm[i] = m
         rows = dot(m, cold_ref[...], 0, 0).astype(BF16)
-        row_send[pl.ds(4 * g, 4)] = rows.reshape(4, IB * REQ, rank)
-        return c
-
-    lax.fori_loop(0, nu // 4, build, 0)
-
-    send_users(row_send, row_recv, 1)
-    row_recv[pl.ds(p, 1)] = row_send[pl.ds(p, 1)]
-    wait_users(row_send, row_recv, 1)
-    for h in range(rank // 128):
-        tab[h, pl.ds(hot_rows, cold_slots * IB), :] = (
-            row_recv[:, :, h * 128 : (h + 1) * 128].reshape(cold_slots * IB, 128).astype(F32)
-        )
+        row_send[c, pl.ds(first, span)] = rows.reshape(span, ROWS, rank)
+        return carry
+
+    def build_and_send(c, carry):
+        lax.fori_loop(c * groups, (c + 1) * groups, build, 0)
+        send_users(row_send.at[c], row_recv.at[c], 8 + c)
+        row_recv[c, pl.ds(p, 1)] = row_send[c, pl.ds(p, 1)]
+        return carry
+
+    lax.fori_loop(0, CH, build_and_send, 0)
 
     hb = jnp.broadcast_to(bh_ref[...], (HB, nblk))
     live = lax.broadcasted_iota(jnp.int32, (HB, nblk), 1) < cnt_ref[0]
 
-    def position(a, c):
-        at = [tab[h, pl.ds(a, slots, stride=IB), :] for h in range(rank // 128)]
+    def position(a, carry):
+        at = [
+            jnp.concatenate(
+                [
+                    hot_tab[h, pl.ds(a, hot_slots, stride=IB), :],
+                    tab[h, pl.ds(a % POS, cold_slots, stride=POS), :],
+                ],
+                axis=0,
+            )
+            for h in range(rank // 128)
+        ]
         items = dot(sel[...], jnp.concatenate(at, axis=1).astype(BF16))
         u = urows[...]
         ui = (u * items).astype(BF16)
@@ -223,25 +241,40 @@
         first = pl.multiple_of(((a // 8) * 2 + a % 2) * hot_slots, hot_slots)
         xs_send[(a % 8) // 2, pl.ds(first, hot_slots), :] = g[:hot_slots].astype(BF16)
         for k in range(rank // 128):
-            cold32[k, pl.ds(a, cold_slots, stride=IB), :] = g[
+            cold32[k, pl.ds(a % POS, cold_slots, stride=POS), :] = g[
                 hot_slots:, k * 128 : (k + 1) * 128
             ]
-        return c
-
-    lax.fori_loop(0, IB, position, 0)
+        return carry
+
+    def chunk(c, carry):
+        wait_users(row_send.at[c], row_recv.at[c], 8 + c)
+        for h in range(rank // 128):
+            tab[h] = row_recv[c, :, :, h * 128 : (h + 1) * 128].astype(F32).reshape(-1, 128)
+        lax.fori_loop(c * POS, (c + 1) * POS, position, 0)
+        for k in range(rank // 128):
+            cold_send[c, :, :, k * 128 : (k + 1) * 128] = (
+                cold32[k].reshape(nu, ROWS, 128).astype(BF16)
+            )
+        cold_recv[c, pl.ds(p, 1)] = cold_send[c, pl.ds(p, 1)]
+
+        @pl.when(c < EARLY)
+        def _():
+            send_cold(c)
+
+        return carry
+
+    def send_cold(c):
+        send_users(cold_send.at[c], cold_recv.at[c], 8 + CH + c)
+
+    lax.fori_loop(0, CH, chunk, 0)
 
     per_q = rank // ni
     hot_q = hot_rows // ni
     xs_send[:, pl.ds(hot_q, per_q), :] = (
         jnp.transpose(hour_acc[...]).astype(BF16).reshape(ni, per_q, rank)
     )
-    for k in range(rank // 128):
-        cold_send[:, :, k * 128 : (k + 1) * 128] = (
-            cold32[k].astype(BF16).reshape(nu, REQ * IB, 128)
-        )
     for k in x_order:
         send_items(xs_send, xs_recv, 2, k)
-    send_users(cold_send, cold_recv, 3, 0, nu // 2)
 
     hi, lo = halves(uterm[...])
     for c in range(ni):
@@ -269,9 +302,9 @@
         for e in range(nu):
             st2_send[e, :, k * 128 : (k + 1) * 128] = st2[k, e : e + 1, :]
     send_users(st2_send, st2_recv, 5)
-    send_users(cold_send, cold_recv, 3, nu // 2, nu - 1)
+    for c in range(EARLY, CH - 1):
+        send_cold(c)
     st2_recv[pl.ds(p, 1)] = st2_send[pl.ds(p, 1)]
-    cold_recv[pl.ds(p, 1)] = cold_send[pl.ds(p, 1)]
     wait_users(st2_send, st2_recv, 5)
     total = st2_recv[0]
     for e in range(1, nu):
@@ -286,6 +319,8 @@
         return c
 
     lax.fori_loop(0, nu - 1, tell, 0)
+    if EARLY < CH:
+        send_cold(CH - 1)
 
     wait_items(user_send, user_recv, 4)
     user_recv[pl.ds(q, 1)] = jnp.zeros((1, udev, rank), BF16)
@@ -299,11 +334,18 @@
         to = (q + k) % ni
         copy_items(hall.at[q], hall.at[q], 7, to).start()
 
-    wait_users(cold_send, cold_recv, 3)
-    acc = jnp.zeros((cold_rows, rank), F32)
-    for g in range(nu // 4):
-        acc = acc + dot(perm[g], cold_recv[pl.ds(4 * g, 4)].reshape(128, rank))
-    cgrad_ref[...] = acc
+    cgrad_ref[...] = jnp.zeros_like(cgrad_ref)
+
+    def collect(c, carry):
+        wait_users(cold_send.at[c], cold_recv.at[c], 8 + CH + c)
+        acc = cgrad_ref[...]
+        for g in range(groups):
+            part = cold_recv[c, pl.ds(span * g, span)].reshape(128, rank)
+            acc = acc + dot(perm[c * groups + g], part)
+        cgrad_ref[...] = acc
+        return carry
+
+    lax.fori_loop(0, CH, collect, 0)
 
     wait_items(hall, hall, 7)
     for c in range(ni):
@@ -353,10 +395,11 @@
             scratch_shapes=[
                 pltpu.VMEM((nu, 1, 128), jnp.int32),
                 pltpu.VMEM((nu, 1, 128), jnp.int32),
-                pltpu.VMEM((nu // 4, cold_rows, 128), BF16),
-                pltpu.VMEM((nu, part, rank), BF16),
-                pltpu.VMEM((nu, part, rank), BF16),
-                pltpu.VMEM((rank // 128, slots * IB, 128), F32),
+                pltpu.VMEM((nu * part // 128, cold_rows, 128), BF16),
+                pltpu.VMEM((CH, nu, ROWS, rank), BF16),
+                pltpu.VMEM((CH, nu, ROWS, rank), BF16),
+                pltpu.VMEM((rank // 128, hot_rows, 128), F32),
+                pltpu.VMEM((rank // 128, nu * ROWS, 128), F32),
                 pltpu.VMEM((nblk, rank), F32),
                 pltpu.VMEM((nblk, slots), BF16),
                 pltpu.VMEM((slots, nblk), BF16),
@@ -364,9 +407,9 @@
                 pltpu.VMEM((IB * HB, nblk), F32),
                 pltpu.VMEM((rank, rank), F32),
                 pltpu.VMEM((nblk, rank), F32),
-                pltpu.VMEM((rank // 128, nu * part, 128), F32),
-                pltpu.VMEM((nu, part, rank), BF16),
-                pltpu.VMEM((nu, part, rank), BF16),
+                pltpu.VMEM((rank // 128, nu * ROWS, 128), F32),
+                pltpu.VMEM((CH, nu, ROWS, rank), BF16),
+                pltpu.VMEM((CH, nu, ROWS, rank), BF16),
                 pltpu.VMEM((ni, udev, rank), F32),
                 pltpu.VMEM((ni, udev, rank), BF16),
                 pltpu.VMEM((ni, udev, rank), BF16),
@@ -377,7 +420,7 @@
                 pltpu.VMEM((nu, 1, 3 * rank), F32),
                 pltpu.VMEM((ni, nu, 1, rank), F32),
                 pltpu.VMEM((rank, rank), F32),
-                pltpu.SemaphoreType.DMA((8, 2)),
+                pltpu.SemaphoreType.DMA((8 + 2 * CH, 2)),
             ],
             compiler_params=pltpu.CompilerParams(
                 collective_id=0, has_side_effects=True, vmem_limit_bytes=56 * 1024 * 1024

time: 114 us -> 90.1 us (0.79); the launches traced: 112 us -> 90 us
  Pallas kernels: 106 us -> 84.1 us
    pallas_call x1, Pallas kernels: 106 us -> 84.1 us  [body(): pl.pallas_call(functools.partial(kernel, nu, ni), out_shape=(jax.ShapeDty...]
where the time goes in v2:
time: 90.1 us; the launch traced here: 90 us
  Pallas kernels  84.1 us (93%)
  local copies, waits for them, and re-layouts  4.59 us (5%)
  between operations  1.32 us (1%)
    pallas_call x1, Pallas kernels, body(): pl.pallas_call(functools.partial(kernel, nu, ni), out_shape=(jax.ShapeDty...  84.1 us
    unnamed x13, local copies, waits for them, and re-layouts  4.59 us

profile of v2, /device:TPU:1, one launch (start us, length us, event | category | flops | bytes accessed | tf_op | source)
XLA Modules:
  0.0 90.0 jit_solution(4905647590287406691)
XLA Ops:
  0.6 0.0 copy-start.3
  1.3 0.0 copy-done.3
  1.3 0.7 copy.14.need_ref
  2.0 84.1 %shard_map.129 = (f32[512,256]{1,0:T(8,128)}, f32[256,256]{1,0:T(8,128)}, f32[2,256]{1,0:T(2,128)}, f32[168,256]{1,0:T(8,128)}) custom-call(bf16[2048,256]{1,0:T(8,128)(2,1)} %user_ref.1, bf16[512,256]{1,0:T(8,128)(2,1)} %hot_ref.1, bf16[256,256]{1,0:T(8,128)(2,1)} %cold_ref.1, bf16[168,256]{1,0:T(8,128)(2,1)} %hour_ref.1, s32[1,512]{1,0:T(1,128)} %bu_ref.1, ...), custom_call_target="tpu_custom_call" | custom-call | tf_op jit(solution)/shard_map/pallas_call | solution.py:385
  86.1 0.0 copy-start
  86.1 1.9 %copy.20 = f32[512,256]{1,0:T(8,128)} copy(f32[512,256]{1,0:T(8,128)} %get-tuple-element.8) | data formatting | bytes 1048576
  88.0 0.0 copy-done
  88.0 0.0 copy-start.2
  88.0 0.0 copy-start.1
  88.0 0.7 copy.21
  88.7 0.0 copy-done.2
  88.7 0.6 copy.22
  89.3 0.0 copy-done.1
  89.3 0.7 copy.23
Async XLA Ops:
  0.6 0.7 copy-start.3
  86.1 1.9 %copy-start = (f32[256,256]{1,0:T(8,128)S(1)}, f32[256,256]{1,0:T(8,128)}, u32[]{:S(2)}) copy-start(f32[256,256]{1,0:T(8,128)} %get-tuple-element.9) | copy-start | bytes 786436
  88.0 0.7 copy-start.2
  88.0 1.3 %copy-start.1 = (f32[168,256]{1,0:T(8,128)S(1)}, f32[168,256]{1,0:T(8,128)}, u32[]{:S(2)}) copy-start(f32[168,256]{1,0:T(8,128)} %get-tuple-element.11) | copy-start | bytes 516100

commit v3 on v2

--- a/solution.py
+++ b/solution.py
@@ -12,7 +12,8 @@
 REQ = 2
 CH = 4
 POS = IB // CH
-EARLY = 2
+EARLY = 3
+UNROLL = 9
 ROWS = REQ * POS
 MESH = pl.DeviceIdType.MESH
 F32 = jnp.float32
@@ -69,8 +70,13 @@
     user32,
     user_send,
     user_recv,
-    xs_send,
-    xs_recv,
+    sel_u,
+    hot_send,
+    hot_recv,
+    hour_send,
+    hour_recv,
+    hrow_send,
+    hrow_recv,
     st2,
     st2_send,
     st2_recv,
@@ -92,9 +98,18 @@
     hour_blocks = hour_count // HB
     hp = hours.shape[0]
 
-    def peer(i):
-        h = i // 2 + 1
-        return (p + h + (i % 2) * (nu - 2 * h)) % nu
+    def each_peer(act):
+        def some(i, c):
+            for j in range(UNROLL):
+                to = p + 1 + i * UNROLL + j
+                act(jnp.where(to >= nu, to - nu, to))
+            return c
+
+        steps = (nu - 1) // UNROLL
+        lax.fori_loop(0, steps, some, 0)
+        for j in range(steps * UNROLL, nu - 1):
+            to = p + 1 + j
+            act(jnp.where(to >= nu, to - nu, to))
 
     def copy_users(src, dst, n, to):
         return pltpu.make_async_remote_copy(
@@ -116,13 +131,8 @@
             device_id_type=MESH,
         )
 
-    def send_users(src, dst, n, lo=0, hi=nu - 1):
-        def one(i, c):
-            to = peer(i)
-            copy_users(src.at[to], dst.at[p], n, to).start()
-            return c
-
-        lax.fori_loop(lo, hi, one, 0)
+    def send_users(src, dst, n):
+        each_peer(lambda to: copy_users(src.at[to], dst.at[p], n, to).start())
 
     def wait_users(src, dst, n):
         d = copy_users(src.at[pl.ds(0, nu - 1)], dst.at[pl.ds(0, nu - 1)], n, (p + 1) % nu)
@@ -142,11 +152,9 @@
 
     barrier = pltpu.get_barrier_semaphore()
 
-    def greet(i, c):
-        pl.semaphore_signal(barrier, inc=1, device_id=(peer(i), q), device_id_type=MESH)
-        return c
-
-    lax.fori_loop(0, nu - 1, greet, 0)
+    each_peer(
+        lambda to: pl.semaphore_signal(barrier, inc=1, device_id=(to, q), device_id_type=MESH)
+    )
     for k in range(1, ni):
         pl.semaphore_signal(barrier, inc=1, device_id=(p, (q + k) % ni), device_id_type=MESH)
 
@@ -167,6 +175,10 @@
     user_col = jnp.transpose(jnp.broadcast_to(bu_ref[...], (8, nblk)))[:, 0:1]
     sel[...] = onehot(lax.broadcasted_iota(jnp.int32, (nblk, slots), 1) == slot_col)
     sel_t[...] = onehot(lax.broadcasted_iota(jnp.int32, (slots, nblk), 0) == bs_ref[...])
+    for c in range(ni):
+        sel_u[c] = onehot(
+            lax.broadcasted_iota(jnp.int32, (udev, nblk), 0) + c * udev == bu_ref[...]
+        )
     urows[...] = jnp.zeros_like(urows)
 
     def pick_user(c, carry):
@@ -238,8 +250,8 @@
         uterm[...] += w * items
         hi, lo = halves(w * u)
         g = dot(sel_t[...], hi) + dot(sel_t[...], lo)
-        first = pl.multiple_of(((a // 8) * 2 + a % 2) * hot_slots, hot_slots)
-        xs_send[(a % 8) // 2, pl.ds(first, hot_slots), :] = g[:hot_slots].astype(BF16)
+        first = pl.multiple_of((a % 2) * hot_slots, hot_slots)
+        hot_send[a // POS, (a % POS) // 2, pl.ds(first, hot_slots), :] = g[:hot_slots].astype(BF16)
         for k in range(rank // 128):
             cold32[k, pl.ds(a % POS, cold_slots, stride=POS), :] = g[
                 hot_slots:, k * 128 : (k + 1) * 128
@@ -261,6 +273,18 @@
         def _():
             send_cold(c)
 
+        half = c // 2
+        for i in range(2):
+            to = 2 * (c % 2) + i
+
+            @pl.when(to != q)
+            def _():
+                copy_items(hot_send.at[c, i], hot_recv.at[half, q], 2 + half, to).start()
+
+            @pl.when(to == q)
+            def _():
+                hot_recv[half, pl.ds(q, 1)] = hot_send[c, pl.ds(i, 1)]
+
         return carry
 
     def send_cold(c):
@@ -269,70 +293,62 @@
     lax.fori_loop(0, CH, chunk, 0)
 
     per_q = rank // ni
-    hot_q = hot_rows // ni
-    xs_send[:, pl.ds(hot_q, per_q), :] = (
-        jnp.transpose(hour_acc[...]).astype(BF16).reshape(ni, per_q, rank)
-    )
+    halves_of = rank // 128
+    hour_send[...] = jnp.transpose(hour_acc[...]).astype(BF16).reshape(ni, per_q, rank)
     for k in x_order:
-        send_items(xs_send, xs_recv, 2, k)
+        send_items(hour_send, hour_recv, 6, k)
+    hour_recv[pl.ds(q, 1)] = hour_send[pl.ds(q, 1)]
 
     hi, lo = halves(uterm[...])
     for c in range(ni):
-        m = onehot(lax.broadcasted_iota(jnp.int32, (udev, nblk), 0) + c * udev == bu_ref[...])
+        m = sel_u[c]
         user32[c] = dot(m, hi) + dot(m, lo)
         user_send[c] = user32[c].astype(BF16)
     for k in x_order:
         send_items(user_send, user_recv, 4, k)
 
-    xs_recv[pl.ds(q, 1)] = xs_send[pl.ds(q, 1)]
-    wait_items(xs_send, xs_recv, 2)
-    x1 = xs_recv[0].astype(F32)
+    wait_items(hour_send, hour_recv, 6)
+    x1 = hour_recv[0].astype(F32)
     for k in range(1, ni):
-        x1 = x1 + xs_recv[k].astype(F32)
+        x1 = x1 + hour_recv[k].astype(F32)
+    for e in range(nu):
+        hrow_send[e] = x1[e : e + 1, :]
+    send_users(hrow_send, hrow_recv, 1)
+    hrow_recv[pl.ds(p, 1)] = hrow_send[pl.ds(p, 1)]
+    for c in range(EARLY, CH):
+        send_cold(c)
+
     for half in range(2):
+        d = copy_items(
+            hot_recv.at[half, pl.ds(0, ni - 1)],
+            hot_recv.at[half, pl.ds(0, ni - 1)],
+            2 + half,
+            (q + 1) % ni,
+        )
+        d.wait_send()
+        d.wait_recv()
+        x1 = hot_recv[half, 0].astype(F32)
+        for k in range(1, ni):
+            x1 = x1 + hot_recv[half, k].astype(F32)
         for j in range(2):
-            first = (half * 2 + j) * hot_slots
-            for k in range(rank // 128):
-                st2[j * (rank // 128) + k, pl.ds(half, hot_slots, stride=2), :] = x1[
-                    first : first + hot_slots, k * 128 : (k + 1) * 128
+            for k in range(halves_of):
+                st2[j * halves_of + k, pl.ds(half, hot_slots, stride=2), :] = x1[
+                    j * hot_slots : (j + 1) * hot_slots, k * 128 : (k + 1) * 128
                 ]
-    for k in range(rank // 128):
-        st2[2 * (rank // 128) + k] = x1[hot_q : hot_q + per_q, k * 128 : (k + 1) * 128]
-    for k in range(3 * rank // 128):
+    for k in range(2 * halves_of):
         for e in range(nu):
             st2_send[e, :, k * 128 : (k + 1) * 128] = st2[k, e : e + 1, :]
+
+    wait_users(hrow_send, hrow_recv, 1)
+    total = hrow_recv[0]
+    for e in range(1, nu):
+        total = total + hrow_recv[e]
+    hall[q, pl.ds(p, 1)] = total.reshape(1, 1, rank)
+
+    mine = hall.at[q, p]
+    each_peer(lambda to: copy_users(mine, mine, 7, to).start())
     send_users(st2_send, st2_recv, 5)
-    for c in range(EARLY, CH - 1):
-        send_cold(c)
     st2_recv[pl.ds(p, 1)] = st2_send[pl.ds(p, 1)]
-    wait_users(st2_send, st2_recv, 5)
-    total = st2_recv[0]
-    for e in range(1, nu):
-        total = total + st2_recv[e]
-    hgrad_ref[pl.ds(0, 1), :] = total[:, :rank]
-    hgrad_ref[pl.ds(1, 1), :] = total[:, rank : 2 * rank]
-    hall[q, pl.ds(p, 1)] = total[:, 2 * rank :].reshape(1, 1, rank)
-
-    def tell(i, c):
-        to = peer(i)
-        copy_users(hall.at[q, p], hall.at[q, p], 6, to).start()
-        return c
-
-    lax.fori_loop(0, nu - 1, tell, 0)
-    if EARLY < CH:
-        send_cold(CH - 1)
-
-    wait_items(user_send, user_recv, 4)
-    user_recv[pl.ds(q, 1)] = jnp.zeros((1, udev, rank), BF16)
-    grad = user32[q]
-    for k in range(ni):
-        grad = grad + user_recv[k].astype(F32)
-    ugrad_ref[...] = grad
-
-    wait_users(hall.at[q], hall.at[q], 6)
-    for k in x_order:
-        to = (q + k) % ni
-        copy_items(hall.at[q], hall.at[q], 7, to).start()
 
     cgrad_ref[...] = jnp.zeros_like(cgrad_ref)
 
@@ -345,13 +361,46 @@
         cgrad_ref[...] = acc
         return carry
 
-    lax.fori_loop(0, CH, collect, 0)
-
-    wait_items(hall, hall, 7)
+    lax.fori_loop(0, CH - 1, collect, 0)
+
+    wait_users(hall.at[q], hall.at[q], 7)
+    for k in x_order:
+        to = (q + k) % ni
+        copy_items(hall.at[q], hall.at[q], 8 + 2 * CH, to).start()
+
+    collect(CH - 1, 0)
+    wait_users(st2_send, st2_recv, 5)
+    total = st2_recv[0]
+    for e in range(1, nu):
+        total = total + st2_recv[e]
+    hgrad_ref[pl.ds(0, 1), :] = total[:, :rank]
+    hgrad_ref[pl.ds(1, 1), :] = total[:, rank : 2 * rank]
+
+    wait_items(user_send, user_recv, 4)
+    user_recv[pl.ds(q, 1)] = jnp.zeros((1, udev, rank), BF16)
+    grad = user32[q]
+    for k in range(ni):
+        grad = grad + user_recv[k].astype(F32)
+    ugrad_ref[...] = grad
+
+    wait_items(hall, hall, 8 + 2 * CH)
     for c in range(ni):
         for e in range(nu):
             hflat[pl.ds(c * nu + e, 1), :] = hall[c, e]
     tgrad_ref[...] = jnp.transpose(hflat[...])[:hour_count, :]
+
+
+def keep(*refs):
+    src, dst, buf, sems = refs[:4], refs[4:8], refs[8:12], refs[12]
+    loads = [pltpu.make_async_copy(src[i], buf[i], sems.at[i, 0]) for i in range(4)]
+    stores = [pltpu.make_async_copy(buf[i], dst[i], sems.at[i, 1]) for i in range(4)]
+    for load in loads:
+        load.start()
+    for load, store in zip(loads, stores):
+        load.wait()
+        store.start()
+    for store in stores:
+        store.wait()
 
 
 def solution(mesh):
@@ -381,8 +430,7 @@
         vmem = pl.BlockSpec(memory_space=pltpu.VMEM)
         specs = [vmem] * 10
         specs[7] = pl.BlockSpec(memory_space=pltpu.SMEM)
-        small = (hot_rows + rank) // ni
-        return pl.pallas_call(
+        results = pl.pallas_call(
             functools.partial(kernel, nu, ni),
             out_shape=(
                 jax.ShapeDtypeStruct((udev, rank), F32),
@@ -413,14 +461,19 @@
                 pltpu.VMEM((ni, udev, rank), F32),
                 pltpu.VMEM((ni, udev, rank), BF16),
                 pltpu.VMEM((ni, udev, rank), BF16),
-                pltpu.VMEM((ni, small, rank), BF16),
-                pltpu.VMEM((ni, small, rank), BF16),
-                pltpu.VMEM((3 * rank // 128, nu, 128), F32),
-                pltpu.VMEM((nu, 1, 3 * rank), F32),
-                pltpu.VMEM((nu, 1, 3 * rank), F32),
+                pltpu.VMEM((ni, udev, nblk), BF16),
+                pltpu.VMEM((CH, 2, 2 * (hot_rows // IB), rank), BF16),
+                pltpu.VMEM((2, ni, 2 * (hot_rows // IB), rank), BF16),
+                pltpu.VMEM((ni, rank // ni, rank), BF16),
+                pltpu.VMEM((ni, rank // ni, rank), BF16),
+                pltpu.VMEM((nu, 1, rank), F32),
+                pltpu.VMEM((nu, 1, rank), F32),
+                pltpu.VMEM((2 * rank // 128, nu, 128), F32),
+                pltpu.VMEM((nu, 1, 2 * rank), F32),
+                pltpu.VMEM((nu, 1, 2 * rank), F32),
                 pltpu.VMEM((ni, nu, 1, rank), F32),
                 pltpu.VMEM((rank, rank), F32),
-                pltpu.SemaphoreType.DMA((8 + 2 * CH, 2)),
+                pltpu.SemaphoreType.DMA((9 + 2 * CH, 2)),
             ],
             compiler_params=pltpu.CompilerParams(
                 collective_id=0, has_side_effects=True, vmem_limit_bytes=56 * 1024 * 1024
@@ -437,6 +490,16 @@
             need_rows,
             observed,
         )
+        shapes = [jax.ShapeDtypeStruct(r.shape, r.dtype) for r in results]
+        anywhere = pl.BlockSpec(memory_space=pl.ANY)
+        return pl.pallas_call(
+            keep,
+            out_shape=shapes,
+            in_specs=[anywhere] * 4,
+            out_specs=[anywhere] * 4,
+            scratch_shapes=[pltpu.VMEM(r.shape, r.dtype) for r in results]
+            + [pltpu.SemaphoreType.DMA((4, 2))],
+        )(*results)
 
     in_specs = (
         P("users", None),

time: 90.1 us -> 83.7 us (0.929)
  local copies, waits for them, and re-layouts: 4.59 us -> 0.72 us
  Pallas kernels: 84.1 us -> 81.5 us
    pallas_call x1, Pallas kernels: 84.1 us -> 79.5 us  [body(): pl.pallas_call(functools.partial(kernel, nu, ni), out_shape=(jax.ShapeDty...]
    unnamed x13 -> x3, local copies, waits for them, and re-layouts: 4.59 us -> 0.72 us
    pallas_call x0 -> x1, Pallas kernels: none -> 2.04 us  [body(): pl.pallas_call(keep, out_shape=shapes, in_specs=[anywhere] * 4, out_specs...]
where the time goes in v3:
time: 83.7 us; the launch traced here: 83.6 us
  Pallas kernels  81.5 us (97%)
  between operations  1.31 us (2%)
    pallas_call x1, Pallas kernels, body(): pl.pallas_call(functools.partial(kernel, nu, ni), out_shape=(jax.ShapeDty...  79.5 us
    pallas_call x1, Pallas kernels, body(): pl.pallas_call(keep, out_shape=shapes, in_specs=[anywhere] * 4, out_specs...  2.04 us

profile of v3, /device:TPU:1, one launch (start us, length us, event | category | flops | bytes accessed | tf_op | source)
XLA Modules:
  0.0 83.6 jit_solution(1523524723823089943)
XLA Ops:
  0.6 0.0 copy-start
  1.3 0.0 copy-done
  1.3 0.7 copy.14.need_ref
  2.0 79.5 %shard_map.129 = (f32[512,256]{1,0:T(8,128)}, f32[256,256]{1,0:T(8,128)}, f32[2,256]{1,0:T(2,128)}, f32[168,256]{1,0:T(8,128)}) custom-call(bf16[2048,256]{1,0:T(8,128)(2,1)} %user_ref.1, bf16[512,256]{1,0:T(8,128)(2,1)} %hot_ref.1, bf16[256,256]{1,0:T(8,128)(2,1)} %cold_ref.1, bf16[168,256]{1,0:T(8,128)(2,1)} %hour_ref.1, s32[1,512]{1,0:T(1,128)} %bu_ref.1, ...), custom_call_target="tpu_custom_call" | custom-call | tf_op jit(solution)/shard_map/pallas_call | solution.py:433
  81.5 2.0 %shard_map.130 = (f32[512,256]{1,0:T(8,128)}, f32[256,256]{1,0:T(8,128)}, f32[2,256]{1,0:T(2,128)}, f32[168,256]{1,0:T(8,128)}) custom-call(f32[512,256]{1,0:T(8,128)} %get-tuple-element.8.refs_0_, f32[256,256]{1,0:T(8,128)} %get-tuple-element.9.refs_1_, f32[2,256]{1,0:T(2,128)} %get-tuple-element.10.refs_2_, f32[168,256]{1,0:T(8,128)} %get-tuple-element.11.refs_3_), custom_call_target="tpu_custom_call" | custom-call | tf_op jit(solution)/shard_map/pallas_call | solution.py:495
Async XLA Ops:
  0.6 0.7 copy-start
